TPU v7x, 32 devices: a whole 2x2x4 slice. The times are simulated.
32 devices in a mesh: dp: 16 (over z, y, core), shard: 2 (over x).
Axes of the slice: x: 2, y: 2, z: 4, core: 2. Of those that a mesh axis runs over, the one named last changes fastest.
Arguments:
- block_input: bfloat16 [4096, 1024], P(('dp', 'shard'))
- out_cotangent: bfloat16 [4096, 1024], P(('dp', 'shard')), may hold values from -6 to 6
- weight_input: float32 [1024, 3072], P('shard', 'dp'), may hold values from -0.1875 to 0.1875
- weight_output: float32 [1024, 1024], P('shard', 'dp'), may hold values from -0.1875 to 0.1875
- weight_gate: float32 [1024, 4608], P('shard', 'dp'), may hold values from -0.1875 to 0.1875
- weight_up: float32 [1024, 4608], P('shard', 'dp'), may hold values from -0.1875 to 0.1875
- weight_down: float32 [4608, 1024], P('shard', 'dp'), may hold values from -0.09375 to 0.09375
- conv_taps: float32 [3, 1024], P(None, 'shard'), may hold values from -3.5 to 3.5
- norm_gains: float32 [2, 1024], P(None, 'shard'), may hold values from 0.5 to 1.5
- first_input: float32 [1024, 3072], P('shard', 'dp'), may hold values from -20 to 20
- first_output: float32 [1024, 1024], P('shard', 'dp'), may hold values from -20 to 20
- first_gate: float32 [1024, 4608], P('shard', 'dp'), may hold values from -20 to 20
- first_up: float32 [1024, 4608], P('shard', 'dp'), may hold values from -20 to 20
- first_down: float32 [4608, 1024], P('shard', 'dp'), may hold values from -20 to 20
- first_taps: float32 [3, 1024], P(None, 'shard'), may hold values from -20 to 20
- first_gains: float32 [2, 1024], P(None, 'shard'), may hold values from -20 to 20
- second_input: float32 [1024, 3072], P('shard', 'dp'), may hold values from 20.48 to 122.88
- second_output: float32 [1024, 1024], P('shard', 'dp'), may hold values from 20.48 to 122.88
- second_gate: float32 [1024, 4608], P('shard', 'dp'), may hold values from 20.48 to 122.88
- second_up: float32 [1024, 4608], P('shard', 'dp'), may hold values from 20.48 to 122.88
- second_down: float32 [4608, 1024], P('shard', 'dp'), may hold values from 20.48 to 122.88
- second_taps: float32 [3, 1024], P(None, 'shard'), may hold values from 20.48 to 122.88
- second_gains: float32 [2, 1024], P(None, 'shard'), may hold values from 20.48 to 122.88
Outputs:
- block_output: bfloat16 [4096, 1024], P(('dp', 'shard'))
- input_gradient: float32 [4096, 1024], P(('dp', 'shard'))
- gradient_input: float32 [1024, 3072], P('shard', 'dp')
- gradient_output: float32 [1024, 1024], P('shard', 'dp')
- gradient_gate: float32 [1024, 4608], P('shard', 'dp')
- gradient_up: float32 [1024, 4608], P('shard', 'dp')
- gradient_down: float32 [4608, 1024], P('shard', 'dp')
- gradient_taps: float32 [3, 1024], P(None, 'shard')
- gradient_gains: float32 [2, 1024], P(None, 'shard')
- updated_input: float32 [1024, 3072], P('shard', 'dp')
- updated_output: float32 [1024, 1024], P('shard', 'dp')
- updated_gate: float32 [1024, 4608], P('shard', 'dp')
- updated_up: float32 [1024, 4608], P('shard', 'dp')
- updated_down: float32 [4608, 1024], P('shard', 'dp')
- updated_taps: float32 [3, 1024], P(None, 'shard')
- updated_gains: float32 [2, 1024], P(None, 'shard')
- moment_input: float32 [1024, 3072], P('shard', 'dp')
- moment_output: float32 [1024, 1024], P('shard', 'dp')
- moment_gate: float32 [1024, 4608], P('shard', 'dp')
- moment_up: float32 [1024, 4608], P('shard', 'dp')
- moment_down: float32 [4608, 1024], P('shard', 'dp')
- moment_taps: float32 [3, 1024], P(None, 'shard')
- moment_gains: float32 [2, 1024], P(None, 'shard')
- square_input: float32 [1024, 3072], P('shard', 'dp')
- square_output: float32 [1024, 1024], P('shard', 'dp')
- square_gate: float32 [1024, 4608], P('shard', 'dp')
- square_up: float32 [1024, 4608], P('shard', 'dp')
- square_down: float32 [4608, 1024], P('shard', 'dp')
- square_taps: float32 [3, 1024], P(None, 'shard')
- square_gains: float32 [2, 1024], P(None, 'shard')
All inputs are finite; a program needn't handle non-finite values.
Results may differ from a plain program's by a relative error of at most 0.00435.
The roundings to bfloat16 on the way count: a program that leaves them out, or rounds other values in their place, can miss the bound.
Values may be sent and summed in bfloat16 or wider, within the bound.
No kernel may reach another device: no remote copies, remote signals or barrier semaphores. Data moves between devices by JAX's collectives and lax.ppermute only.
A program may use at most 320 MiB of HBM per device.

v0:
```python
import jax
import jax.numpy as jnp
from jax import lax
from jax.sharding import PartitionSpec as P

D = 1024
KCONV = 3
LEN = 128
STEP = 10
epsilon_norm = 1e-05
epsilon_adam = 1e-08
beta_first = 0.9
beta_second = 0.95
rate_matrix = 0.01
rate_vector = 0.1
weight_decay = 0.1


def product(left, right):
    return jnp.dot(left, right, preferred_element_type=jnp.float32)


def times_transposed(left, right):
    return lax.dot_general(
        left, right, (((1,), (1,)), ((), ())), preferred_element_type=jnp.float32
    )


def transposed_times(left, right):
    return lax.dot_general(
        left, right, (((0,), (0,)), ((), ())), preferred_element_type=jnp.float32
    )


def delayed(values, steps):
    seqs = values.reshape(-1, LEN, values.shape[-1])
    padded = jnp.pad(seqs, ((0, 0), (steps, 0), (0, 0)))[:, :LEN]
    return padded.reshape(values.shape)


def advanced(values, steps):
    seqs = values.reshape(-1, LEN, values.shape[-1])
    padded = jnp.pad(seqs, ((0, 0), (0, steps), (0, 0)))[:, steps:]
    return padded.reshape(values.shape)


def norm_scale(values):
    return lax.rsqrt(jnp.mean(values * values, axis=1, keepdims=True) + epsilon_norm)


def norm_back(grad_in, normed, scale, gain):
    weighted = grad_in * gain
    return scale * (weighted - normed * jnp.mean(weighted * normed, axis=1, keepdims=True))


def reduce_weight(left, right):
    owned = lax.psum_scatter(
        transposed_times(left, right), "shard", scatter_dimension=0, tiled=True
    )
    return lax.psum_scatter(owned, "dp", scatter_dimension=1, tiled=True)


def adam_step(param, grad, moment, square, rate, decay):
    moment_new = beta_first * moment + (1.0 - beta_first) * grad
    square_new = beta_second * square + (1.0 - beta_second) * grad * grad
    corrected = moment_new / (1.0 - beta_first**STEP)
    spread = jnp.sqrt(square_new / (1.0 - beta_second**STEP))
    updated = param - rate * (corrected / (spread + epsilon_adam) + decay * param)
    return (updated, moment_new, square_new)


def shards(
    block_input,
    out_cotangent,
    weight_input,
    weight_output,
    weight_gate,
    weight_up,
    weight_down,
    conv_taps,
    norm_gains,
    first_input,
    first_output,
    first_gate,
    first_up,
    first_down,
    first_taps,
    first_gains,
    second_input,
    second_output,
    second_gate,
    second_up,
    second_down,
    second_taps,
    second_gains,
):
    columns = (
        lax.all_gather(weight_input.astype(jnp.bfloat16), "dp", axis=1, tiled=True),
        lax.all_gather(weight_output.astype(jnp.bfloat16), "dp", axis=1, tiled=True),
        lax.all_gather(weight_gate.astype(jnp.bfloat16), "dp", axis=1, tiled=True),
        lax.all_gather(weight_up.astype(jnp.bfloat16), "dp", axis=1, tiled=True),
        lax.all_gather(weight_down.astype(jnp.bfloat16), "dp", axis=1, tiled=True),
    )
    values = block_input.astype(jnp.float32)
    scale_one = norm_scale(values)
    normed_one = values * scale_one
    whole_input, whole_output, whole_gate, whole_up, whole_down, whole_taps, whole_gains = (
        lax.all_gather(columns[0], "shard", axis=0, tiled=True),
        lax.all_gather(columns[1], "shard", axis=0, tiled=True),
        lax.all_gather(columns[2], "shard", axis=0, tiled=True),
        lax.all_gather(columns[3], "shard", axis=0, tiled=True),
        lax.all_gather(columns[4], "shard", axis=0, tiled=True),
        lax.all_gather(conv_taps.astype(jnp.bfloat16), "shard", axis=1, tiled=True),
        lax.all_gather(norm_gains.astype(jnp.bfloat16), "shard", axis=1, tiled=True),
    )
    gains = whole_gains.astype(jnp.float32)
    taps = whole_taps.astype(jnp.float32)
    hidden_one = (normed_one * gains[0]).astype(jnp.bfloat16)
    projected = product(hidden_one, whole_input)
    input_gate = projected[:, :D]
    output_gate = projected[:, D : 2 * D]
    mixer_values = projected[:, 2 * D :]
    mixed_in = input_gate * mixer_values
    shifted = [delayed(mixed_in, step) for step in range(KCONV)]
    conv_out = taps[0] * shifted[0]
    for step in range(1, KCONV):
        conv_out = conv_out + taps[step] * shifted[step]
    gated = (output_gate * conv_out).astype(jnp.bfloat16)
    residual = values + product(gated, whole_output)
    scale_two = norm_scale(residual)
    normed_two = residual * scale_two
    hidden_two = (normed_two * gains[1]).astype(jnp.bfloat16)
    gate_pre = product(hidden_two, whole_gate)
    up_pre = product(hidden_two, whole_up)
    sigmoid_gate = jax.nn.sigmoid(gate_pre)
    silu_gate = gate_pre * sigmoid_gate
    activated = (silu_gate * up_pre).astype(jnp.bfloat16)
    block_output = (residual + product(activated, whole_down)).astype(jnp.bfloat16)
    act_grad = times_transposed(out_cotangent, whole_down)
    grad_down = reduce_weight(activated, out_cotangent)
    gate_grad = (act_grad * up_pre * sigmoid_gate * (1.0 + gate_pre * (1.0 - sigmoid_gate))).astype(
        jnp.bfloat16
    )
    up_grad = (act_grad * silu_gate).astype(jnp.bfloat16)
    grad_gate = reduce_weight(hidden_two, gate_grad)
    grad_up = reduce_weight(hidden_two, up_grad)
    hidden_two_grad = times_transposed(gate_grad, whole_gate) + times_transposed(up_grad, whole_up)
    gain_two_grad = jnp.sum(hidden_two_grad * normed_two, axis=0)
    residual_grad = out_cotangent.astype(jnp.float32) + norm_back(
        hidden_two_grad, normed_two, scale_two, gains[1]
    )
    residual_half = residual_grad.astype(jnp.bfloat16)
    grad_output = reduce_weight(gated, residual_half)
    gated_grad = times_transposed(residual_half, whole_output)
    conv_grad = gated_grad * output_gate
    mixed_grad = taps[0] * conv_grad
    for step in range(1, KCONV):
        mixed_grad = mixed_grad + taps[step] * advanced(conv_grad, step)
    taps_grad = jnp.stack([jnp.sum(conv_grad * shifted[step], axis=0) for step in range(KCONV)], 0)
    projected_grad = jnp.concatenate(
        [mixed_grad * mixer_values, gated_grad * conv_out, mixed_grad * input_gate], axis=1
    ).astype(jnp.bfloat16)
    grad_input = reduce_weight(hidden_one, projected_grad)
    hidden_one_grad = times_transposed(projected_grad, whole_input)
    gain_one_grad = jnp.sum(hidden_one_grad * normed_one, axis=0)
    input_gradient = residual_grad + norm_back(hidden_one_grad, normed_one, scale_one, gains[0])
    vector_terms = jnp.concatenate(
        [taps_grad, gain_one_grad[None, :], gain_two_grad[None, :]], axis=0
    )
    vector_owned = lax.psum_scatter(vector_terms, "shard", scatter_dimension=1, tiled=True)
    vector_total = lax.psum(vector_owned, "dp")
    grad_taps = vector_total[:KCONV]
    grad_gains = vector_total[KCONV:]
    params = (
        weight_input,
        weight_output,
        weight_gate,
        weight_up,
        weight_down,
        conv_taps,
        norm_gains,
    )
    grads = (grad_input, grad_output, grad_gate, grad_up, grad_down, grad_taps, grad_gains)
    firsts = (first_input, first_output, first_gate, first_up, first_down, first_taps, first_gains)
    seconds = (
        second_input,
        second_output,
        second_gate,
        second_up,
        second_down,
        second_taps,
        second_gains,
    )
    updated = []
    moments = []
    squares = []
    for index in range(7):
        rate = rate_matrix if index < 5 else rate_vector
        decay = weight_decay if index < 5 else 0.0
        result = adam_step(params[index], grads[index], firsts[index], seconds[index], rate, decay)
        updated.append(result[0])
        moments.append(result[1])
        squares.append(result[2])
    return (
        block_output,
        input_gradient,
        grads[0],
        grads[1],
        grads[2],
        grads[3],
        grads[4],
        grads[5],
        grads[6],
        updated[0],
        updated[1],
        updated[2],
        updated[3],
        updated[4],
        updated[5],
        updated[6],
        moments[0],
        moments[1],
        moments[2],
        moments[3],
        moments[4],
        moments[5],
        moments[6],
        squares[0],
        squares[1],
        squares[2],
        squares[3],
        squares[4],
        squares[5],
        squares[6],
    )


def solution(mesh):
    placed = (
        P(("dp", "shard"), None),
        P(("dp", "shard"), None),
        P("shard", "dp"),
        P("shard", "dp"),
        P("shard", "dp"),
        P("shard", "dp"),
        P("shard", "dp"),
        P(None, "shard"),
        P(None, "shard"),
        P("shard", "dp"),
        P("shard", "dp"),
        P("shard", "dp"),
        P("shard", "dp"),
        P("shard", "dp"),
        P(None, "shard"),
        P(None, "shard"),
        P("shard", "dp"),
        P("shard", "dp"),
        P("shard", "dp"),
        P("shard", "dp"),
        P("shard", "dp"),
        P(None, "shard"),
        P(None, "shard"),
    )
    return jax.shard_map(
        shards,
        mesh=mesh,
        in_specs=placed,
        out_specs=(
            P(("dp", "shard"), None),
            P(("dp", "shard"), None),
            P("shard", "dp"),
            P("shard", "dp"),
            P("shard", "dp"),
            P("shard", "dp"),
            P("shard", "dp"),
            P(None, "shard"),
            P(None, "shard"),
            P("shard", "dp"),
            P("shard", "dp"),
            P("shard", "dp"),
            P("shard", "dp"),
            P("shard", "dp"),
            P(None, "shard"),
            P(None, "shard"),
            P("shard", "dp"),
            P("shard", "dp"),
            P("shard", "dp"),
            P("shard", "dp"),
            P("shard", "dp"),
            P(None, "shard"),
            P(None, "shard"),
            P("shard", "dp"),
            P("shard", "dp"),
            P("shard", "dp"),
            P("shard", "dp"),
            P("shard", "dp"),
            P(None, "shard"),
            P(None, "shard"),
        ),
        check_vma=False,
    )
```

profile of v0, /device:TPU:0, one launch (start us, length us, event | category | flops | bytes accessed | tf_op | source)
XLA Modules:
  0.0 2118.9 jit_solution(6194754667816132566)
XLA Ops:
  14.3 44.8 %all-gather.11.cloned.1.call-done = bf16[512,3072]{0,1:T(8,128)(2,1)} async-done(((bf16[512,192]{0,1:T(8,128)(2,1)}), bf16[512,3072]{0,1:T(8,128)(2,1)}) %all-gather.11.cloned.1.call-update) | async-done | bytes 3145744 | tf_op jit(solution)/shard_map/all_gather | solution.py:98
  59.2 38.9 %all-gather.15.cloned.1.call-done = bf16[512,1024]{0,1:T(8,128)(2,1)} async-done(((bf16[512,64]{0,1:T(8,128)(2,1)}), bf16[512,1024]{0,1:T(8,128)(2,1)}) %all-gather.15.cloned.1.call-update) | async-done | bytes 1048592 | tf_op jit(solution)/shard_map/all_gather | solution.py:99
  98.1 54.9 %all-gather.23.cloned.1.call-done = bf16[512,4608]{0,1:T(8,128)(2,1)} async-done(((bf16[512,288]{0,1:T(8,128)(2,1)}), bf16[512,4608]{0,1:T(8,128)(2,1)}) %all-gather.23.cloned.1.call-update) | async-done | bytes 4718608 | tf_op jit(solution)/shard_map/all_gather | solution.py:101
  153.1 54.3 %all-gather.19.cloned.1.call-done = bf16[512,4608]{0,1:T(8,128)(2,1)} async-done(((bf16[512,288]{0,1:T(8,128)(2,1)}), bf16[512,4608]{0,1:T(8,128)(2,1)}) %all-gather.19.cloned.1.call-update) | async-done | bytes 4718608 | tf_op jit(solution)/shard_map/all_gather | solution.py:100
  207.5 54.3 %all-gather.27.cloned.1.call-done = bf16[2304,1024]{0,1:T(8,128)(2,1)} async-done(((bf16[2304,64]{0,1:T(8,128)(2,1)}), bf16[2304,1024]{0,1:T(8,128)(2,1)}) %all-gather.27.cloned.1.call-update) | async-done | bytes 4718608 | tf_op jit(solution)/shard_map/all_gather | solution.py:102
  271.5 70.7 %all-gather.13.cloned.1.call-done = bf16[1024,3072]{0,1:T(8,128)(2,1)} async-done(((bf16[512,3072]{0,1:T(8,128)(2,1)}), bf16[1024,3072]{0,1:T(8,128)(2,1)}) %all-gather.13.cloned.1.call-update) | async-done | bytes 6291472 | tf_op jit(solution)/shard_map/all_gather | solution.py:108
  349.1 27.8 %all-gather.17.cloned.1.call-done = bf16[1024,1024]{0,1:T(8,128)(2,1)} async-done(((bf16[512,1024]{0,1:T(8,128)(2,1)}), bf16[1024,1024]{0,1:T(8,128)(2,1)}) %all-gather.17.cloned.1.call-update) | async-done | bytes 2097168 | tf_op jit(solution)/shard_map/all_gather | solution.py:109
  379.5 116.9 %all-gather.25.cloned.1.call-done = bf16[1024,4608]{0,1:T(8,128)(2,1)} async-done(((bf16[512,4608]{0,1:T(8,128)(2,1)}), bf16[1024,4608]{0,1:T(8,128)(2,1)}) %all-gather.25.cloned.1.call-update) | async-done | bytes 9437200 | tf_op jit(solution)/shard_map/all_gather | solution.py:111
  496.4 8.3 fusion.51
  504.7 111.3 %all-gather.21.cloned.1.call-done = bf16[1024,4608]{0,1:T(8,128)(2,1)} async-done(((bf16[512,4608]{0,1:T(8,128)(2,1)}), bf16[1024,4608]{0,1:T(8,128)(2,1)}) %all-gather.21.cloned.1.call-update) | async-done | bytes 9437200 | tf_op jit(solution)/shard_map/all_gather | solution.py:110
  616.0 8.3 fusion.50
  624.3 111.1 %all-gather.29.cloned.1.call-done = bf16[4608,1024]{0,1:T(8,128)(2,1)} async-done(((bf16[2304,1024]{0,1:T(8,128)(2,1)}), bf16[4608,1024]{0,1:T(8,128)(2,1)}) %all-gather.29.cloned.1.call-update) | async-done | bytes 9437200 | tf_op jit(solution)/shard_map/all_gather | solution.py:112
  735.4 8.5 multiply_convert_fusion
  757.5 6.5 fusion.25
  765.3 7.9 fusion.54
  774.7 8.1 fusion.55
  782.9 8.0 fusion.53
  796.8 10.8 reduce-scatter.24.cloned.1.call-done
  810.6 143.7 %reduce-scatter.22.cloned.1.call-done = f32[512,3072]{1,0:T(8,128)} async-done(((f32[1024,3072]{1,0:T(8,128)}), f32[512,3072]{1,0:T(8,128)}) %reduce-scatter.22.cloned.1.call-update) | async-done | bytes 6291472 | tf_op jit(solution)/shard_map/reduce_scatter | solution.py:57
  954.3 6.6 copy.153
  960.9 207.5 %reduce-scatter.28.cloned.1.call-done = f32[512,4608]{1,0:T(8,128)} async-done(((f32[1024,4608]{1,0:T(8,128)}), f32[512,4608]{1,0:T(8,128)}) %reduce-scatter.28.cloned.1.call-update) | async-done | bytes 9437200 | tf_op jit(solution)/shard_map/reduce_scatter | solution.py:57
  1168.4 9.6 copy.159
  1178.1 204.3 %reduce-scatter.30.cloned.1.call-done = f32[2304,1024]{1,0:T(8,128)} async-done(((f32[4608,1024]{1,0:T(8,128)}), f32[2304,1024]{1,0:T(8,128)}) %reduce-scatter.30.cloned.1.call-update) | async-done | bytes 9437200 | tf_op jit(solution)/shard_map/reduce_scatter | solution.py:57
  1382.4 9.7 copy.161
  1392.3 204.0 %reduce-scatter.26.cloned.1.call-done = f32[512,4608]{1,0:T(8,128)} async-done(((f32[1024,4608]{1,0:T(8,128)}), f32[512,4608]{1,0:T(8,128)}) %reduce-scatter.26.cloned.1.call-update) | async-done | bytes 9437200 | tf_op jit(solution)/shard_map/reduce_scatter | solution.py:57
  1596.3 9.6 copy.157
  1608.0 7.6 fusion.1
  1615.7 61.4 %psum.7 = f32[5,512]{1,0:T(8,128)S(1)} all-reduce(f32[5,512]{1,0:T(8,128)} %reduce-scatter.32.cloned.1.call-done), channel_id=1, replica_groups=mesh['dp'=16,'shard'=2] {'dp'}, use_global_device_ids=true, to_apply=%region_20.21 | all-reduce | flops 2560 | bytes 20480 | tf_op jit(solution)/shard_map/psum | solution.py:171
  1680.1 83.4 %reduce-scatter.34.cloned.1.call-done = f32[192,512]{1,0:T(8,128)} async-done(((f32[3072,512]{1,0:T(8,128)}), f32[192,512]{1,0:T(8,128)}) %reduce-scatter.34.cloned.1.call-update) | async-done | bytes 393232
  1765.7 112.8 %reduce-scatter.40.cloned.1.call-done = f32[288,512]{1,0:T(8,128)} async-done(((f32[4608,512]{1,0:T(8,128)}), f32[288,512]{1,0:T(8,128)}) %reduce-scatter.40.cloned.1.call-update) | async-done | bytes 589840
  1881.1 112.8 %reduce-scatter.42.cloned.1.call-done = f32[64,2304]{1,0:T(8,128)} async-done(((f32[1024,2304]{1,0:T(8,128)}), f32[64,2304]{1,0:T(8,128)}) %reduce-scatter.42.cloned.1.call-update) | async-done | bytes 589840
  1996.5 113.0 %reduce-scatter.38.cloned.1.call-done = f32[288,512]{1,0:T(8,128)} async-done(((f32[4608,512]{1,0:T(8,128)}), f32[288,512]{1,0:T(8,128)}) %reduce-scatter.38.cloned.1.call-update) | async-done | bytes 589840
  (204 shorter events, 66.8 us)
Async XLA Ops:
  7.2 51.9 %all-gather.11.cloned.1.call-start = ((), (), s32[]{:S(2)}) async-start(), calls=%async_computation.11 | async-start | bytes 3342336 | tf_op jit(solution)/shard_map/all_gather | solution.py:98
  9.1 89.0 %all-gather.15.cloned.1.call-start = ((), (), s32[]{:S(2)}) async-start(), calls=%async_computation.13 | async-start | bytes 1114112 | tf_op jit(solution)/shard_map/all_gather | solution.py:99
  10.7 142.4 %all-gather.23.cloned.1.call-start = ((), (), s32[]{:S(2)}) async-start(), calls=%async_computation.17 | async-start | bytes 5013504 | tf_op jit(solution)/shard_map/all_gather | solution.py:101
  12.6 194.9 %all-gather.19.cloned.1.call-start = ((), (), s32[]{:S(2)}) async-start(), calls=%async_computation.15 | async-start | bytes 5013504 | tf_op jit(solution)/shard_map/all_gather | solution.py:100
  13.4 248.4 %all-gather.27.cloned.1.call-start = ((), (), s32[]{:S(2)}) async-start(), calls=%async_computation.19 | async-start | bytes 5013504 | tf_op jit(solution)/shard_map/all_gather | solution.py:102
  14.3 327.9 %all-gather.13.cloned.1.call-start = ((), (), s32[]{:S(2)}) async-start(), calls=%async_computation.12 | async-start | bytes 9437184 | tf_op jit(solution)/shard_map/all_gather | solution.py:108
  59.1 317.7 %all-gather.17.cloned.1.call-start = ((), (), s32[]{:S(2)}) async-start(), calls=%async_computation.14 | async-start | bytes 3145728 | tf_op jit(solution)/shard_map/all_gather | solution.py:109
  98.1 398.3 %all-gather.25.cloned.1.call-start = ((), (), s32[]{:S(2)}) async-start(), calls=%async_computation.18 | async-start | bytes 14155776 | tf_op jit(solution)/shard_map/all_gather | solution.py:111
  153.1 462.9 %all-gather.21.cloned.1.call-start = ((), (), s32[]{:S(2)}) async-start(), calls=%async_computation.16 | async-start | bytes 14155776 | tf_op jit(solution)/shard_map/all_gather | solution.py:110
  207.5 527.9 %all-gather.29.cloned.1.call-start = ((), (), s32[]{:S(2)}) async-start(), calls=%async_computation.20 | async-start | bytes 14155776 | tf_op jit(solution)/shard_map/all_gather | solution.py:112
  261.9 545.7 %reduce-scatter.24.cloned.1.call-start = ((), (), s32[]{:S(2)}) async-start(), calls=%async_computation.22 | async-start | bytes 6291456 | tf_op jit(solution)/shard_map/reduce_scatter | solution.py:57
  349.1 155.7 %copy-start.16 = (bf16[128,1024]{1,0:T(8,128)(2,1)}, bf16[128,1024]{1,0:T(8,128)(2,1)S(1)}, u32[]{:S(2)}) copy-start(bf16[128,1024]{1,0:T(8,128)(2,1)S(1)} %get-tuple-element.153) | copy-start | bytes 786436
  753.0 201.3 %reduce-scatter.22.cloned.1.call-start = ((), (), s32[]{:S(2)}) async-start(), calls=%async_computation.21 | async-start | bytes 18874368 | tf_op jit(solution)/shard_map/reduce_scatter | solution.py:57
  764.1 404.3 %reduce-scatter.28.cloned.1.call-start = ((), (), s32[]{:S(2)}) async-start(), calls=%async_computation.24 | async-start | bytes 28311552 | tf_op jit(solution)/shard_map/reduce_scatter | solution.py:57
  773.3 609.0 %reduce-scatter.30.cloned.1.call-start = ((), (), s32[]{:S(2)}) async-start(), calls=%async_computation.25 | async-start | bytes 28311552 | tf_op jit(solution)/shard_map/reduce_scatter | solution.py:57
  782.8 813.5 %reduce-scatter.26.cloned.1.call-start = ((), (), s32[]{:S(2)}) async-start(), calls=%async_computation.23 | async-start | bytes 28311552 | tf_op jit(solution)/shard_map/reduce_scatter | solution.py:57
  791.0 824.7 %reduce-scatter.32.cloned.1.call-start = ((), (), s32[]{:S(2)}) async-start(), calls=%async_computation.26 | async-start | bytes 49152 | tf_op jit(solution)/shard_map/reduce_scatter | solution.py:170
  796.7 881.7 %reduce-scatter.36.cloned.1.call-start = ((), (), s32[]{:S(2)}) async-start(), calls=%async_computation.28 | async-start | bytes 2228224
  810.6 952.9 %reduce-scatter.34.cloned.1.call-start = ((), (), s32[]{:S(2)}) async-start(), calls=%async_computation.27 | async-start | bytes 6684672
  960.9 917.6 %reduce-scatter.40.cloned.1.call-start = ((), (), s32[]{:S(2)}) async-start(), calls=%async_computation.30 | async-start | bytes 10027008
  1178.0 815.9 %reduce-scatter.42.cloned.1.call-start = ((), (), s32[]{:S(2)}) async-start(), calls=%async_computation.31 | async-start | bytes 10027008
  1392.0 717.5 %reduce-scatter.38.cloned.1.call-start = ((), (), s32[]{:S(2)}) async-start(), calls=%async_computation.29 | async-start | bytes 10027008
  1608.0 155.5 %copy-start.18 = (f32[512,192]{0,1:T(8,128)S(1)}, f32[512,192]{0,1:T(8,128)}, u32[]{:S(2)}) copy-start(f32[512,192]{0,1:T(8,128)} %param.25) | copy-start | bytes 1179652
  1615.7 262.9 %copy-start.11 = (f32[512,288]{0,1:T(8,128)S(1)}, f32[512,288]{0,1:T(8,128)}, u32[]{:S(2)}) copy-start(f32[512,288]{0,1:T(8,128)} %param.28) | copy-start | bytes 1769476
  1615.7 262.9 %copy-start.27 = (f32[512,288]{0,1:T(8,128)S(1)}, f32[512,288]{0,1:T(8,128)}, u32[]{:S(2)}) copy-start(f32[512,288]{0,1:T(8,128)} %param.35) | copy-start | bytes 1769476
  1615.7 262.9 %copy-start.28 = (f32[512,288]{0,1:T(8,128)S(1)}, f32[512,288]{0,1:T(8,128)}, u32[]{:S(2)}) copy-start(f32[512,288]{0,1:T(8,128)} %param.42) | copy-start | bytes 1769476
  1765.7 228.2 %copy-start.13 = (f32[2304,64]{0,1:T(8,128)S(1)}, f32[2304,64]{0,1:T(8,128)}, u32[]{:S(2)}) copy-start(f32[2304,64]{0,1:T(8,128)} %param.29) | copy-start | bytes 1769476
  1765.7 228.2 %copy-start.29 = (f32[2304,64]{0,1:T(8,128)S(1)}, f32[2304,64]{0,1:T(8,128)}, u32[]{:S(2)}) copy-start(f32[2304,64]{0,1:T(8,128)} %param.36) | copy-start | bytes 1769476
  1765.7 228.2 %copy-start.30 = (f32[2304,64]{0,1:T(8,128)S(1)}, f32[2304,64]{0,1:T(8,128)}, u32[]{:S(2)}) copy-start(f32[2304,64]{0,1:T(8,128)} %param.43) | copy-start | bytes 1769476
  1881.1 228.4 %copy-start.15 = (f32[512,288]{0,1:T(8,128)S(1)}, f32[512,288]{0,1:T(8,128)}, u32[]{:S(2)}) copy-start(f32[512,288]{0,1:T(8,128)} %param.27) | copy-start | bytes 1769476
  1881.1 228.4 %copy-start.31 = (f32[512,288]{0,1:T(8,128)S(1)}, f32[512,288]{0,1:T(8,128)}, u32[]{:S(2)}) copy-start(f32[512,288]{0,1:T(8,128)} %param.34) | copy-start | bytes 1769476
  1881.1 228.4 %copy-start.32 = (f32[512,288]{0,1:T(8,128)S(1)}, f32[512,288]{0,1:T(8,128)}, u32[]{:S(2)}) copy-start(f32[512,288]{0,1:T(8,128)} %param.41) | copy-start | bytes 1769476
  (49 other events, 1321.9 us)
Sparse Core Ops, SparseCore 0:
  10.9 48.1 all-gather.10
  61.8 36.1 all-gather.14
  100.9 52.0 all-gather.22
  155.8 51.6 all-gather.18
  210.2 51.6 all-gather.26
  263.3 78.8 all-gather.12
  343.7 33.0 all-gather.16
  378.4 117.9 all-gather.24
  498.0 117.9 all-gather.20
  617.4 117.9 all-gather.28
  753.2 54.3 reduce-scatter.23
  809.7 144.5 reduce-scatter.21
  956.6 211.7 reduce-scatter.27
  1170.6 211.7 reduce-scatter.29
  1384.5 211.7 reduce-scatter.25
  1598.9 9.9 reduce-scatter.31
  1613.1 62.0 reduce-scatter.35
  1679.5 83.9 reduce-scatter.33
  1768.2 110.3 reduce-scatter.39
  1883.1 110.8 reduce-scatter.41
  1998.6 110.8 reduce-scatter.37
where the time goes:
time: 2120 us
  waiting for transfers between devices  1880 us (89%)
  matrix products  84.4 us (4%)
  blocking collectives  70.1 us (3%)
  local copies, waits for them, and re-layouts  48.5 us (2%)
  other arithmetic  22.4 us (1%)
    reduce_scatter x5, waiting for transfers between devices, reduce_weight(): lax.psum_scatter(transposed_times(left, right), 'shard', scatter_dimensio...  770 us
    unnamed x26, waiting for transfers between devices  422 us
    all_gather x1, waiting for transfers between devices, shards(): lax.all_gather(columns[3], 'shard', axis=0, tiled=True)  117 us
    all_gather x1, waiting for transfers between devices, shards(): lax.all_gather(columns[2], 'shard', axis=0, tiled=True)  111 us
    all_gather x1, waiting for transfers between devices, shards(): lax.all_gather(columns[4], 'shard', axis=0, tiled=True)  111 us
    all_gather x1, waiting for transfers between devices, shards(): lax.all_gather(columns[0], 'shard', axis=0, tiled=True)  70.7 us
    psum x1, blocking collectives, shards(): vector_total = lax.psum(vector_owned, 'dp')  61.4 us
    all_gather x1, waiting for transfers between devices, shards(): lax.all_gather(weight_up.astype(jnp.bfloat16), 'dp', axis=1, tiled=True)  54.9 us
  transfers between devices with their start and end apart: 21, of which 19 were waited for; matrix products, arithmetic and copies ran while one was open for 6% of the time, Pallas kernels for 0%

commit v1 on v0

--- a/solution.py
+++ b/solution.py
@@ -14,6 +14,18 @@
 rate_matrix = 0.01
 rate_vector = 0.1
 weight_decay = 0.1
+
+
+def doubled_up(shard, axis, dim):
+    ways, here, step = (lax.axis_size(axis), lax.axis_index(axis), shard.shape[dim])
+    line, have = (shard, 1)
+    while have < ways:
+        line = jnp.concatenate(
+            [line, lax.ppermute(line, axis, [(d, (d - have) % ways) for d in range(ways)])],
+            axis=dim,
+        )
+        have = 2 * have
+    return jnp.roll(line, here * step, axis=dim)
 
 
 def product(left, right):
@@ -108,7 +120,7 @@
         lax.all_gather(columns[0], "shard", axis=0, tiled=True),
         lax.all_gather(columns[1], "shard", axis=0, tiled=True),
         lax.all_gather(columns[2], "shard", axis=0, tiled=True),
-        lax.all_gather(columns[3], "shard", axis=0, tiled=True),
+        doubled_up(columns[3], "shard", 0),
         lax.all_gather(columns[4], "shard", axis=0, tiled=True),
         lax.all_gather(conv_taps.astype(jnp.bfloat16), "shard", axis=1, tiled=True),
         lax.all_gather(norm_gains.astype(jnp.bfloat16), "shard", axis=1, tiled=True),

time: 2120 us -> 2090 us (0.986)
  waiting for transfers between devices: 1880 us -> 1650 us
  blocking collectives: 70.1 us -> 249 us
    all_gather x1, blocking collectives: 4.35 us -> 183 us  [shards(): lax.all_gather(norm_gains.astype(jnp.bfloat16), 'shard', axis=1, tiled=True)]
    all_gather x1 -> x0, waiting for transfers between devices: 117 us -> none  [shards(): lax.all_gather(columns[3], 'shard', axis=0, tiled=True)]
    all_gather x1, waiting for transfers between devices: 70.7 us -> 0.02 us  [shards(): lax.all_gather(columns[0], 'shard', axis=0, tiled=True)]
    all_gather x1, waiting for transfers between devices: 27.8 us -> 0.01 us  [shards(): lax.all_gather(columns[1], 'shard', axis=0, tiled=True)]
    unnamed x125 -> x117, local copies, waits for them, and re-layouts: 47.8 us -> 44.9 us
    unnamed x26 -> x25, waiting for transfers between devices: 422 us -> 422 us
  transfers between devices with their start and end apart: 21 -> 21, of which waited for: 19 -> 16; matrix products, arithmetic and copies ran while one was open for 6% -> 6% of each run, Pallas kernels for 0% -> 0%
where the time goes in v1:
time: 2090 us
  waiting for transfers between devices  1650 us (79%)
  blocking collectives  249 us (12%)
  matrix products  87.4 us (4%)
  local copies, waits for them, and re-layouts  45.5 us (2%)
  other arithmetic  35.5 us (2%)
    reduce_scatter x5, waiting for transfers between devices, reduce_weight(): lax.psum_scatter(transposed_times(left, right), 'shard', scatter_dimensio...  771 us
    unnamed x25, waiting for transfers between devices  422 us
    all_gather x1, blocking collectives, shards(): lax.all_gather(norm_gains.astype(jnp.bfloat16), 'shard', axis=1, tiled=True)  183 us
    all_gather x1, waiting for transfers between devices, shards(): lax.all_gather(columns[4], 'shard', axis=0, tiled=True)  111 us
    all_gather x1, waiting for transfers between devices, shards(): lax.all_gather(columns[2], 'shard', axis=0, tiled=True)  101 us
    psum x1, blocking collectives, shards(): vector_total = lax.psum(vector_owned, 'dp')  61.4 us
    all_gather x1, waiting for transfers between devices, shards(): lax.all_gather(weight_gate.astype(jnp.bfloat16), 'dp', axis=1, tiled=True)  54.9 us
    all_gather x1, waiting for transfers between devices, shards(): lax.all_gather(weight_down.astype(jnp.bfloat16), 'dp', axis=1, tiled=True)  54.3 us
  transfers between devices with their start and end apart: 21, of which 16 were waited for; matrix products, arithmetic and copies ran while one was open for 6% of the time, Pallas kernels for 0%

profile of v1, /device:TPU:0, one launch (start us, length us, event | category | flops | bytes accessed | tf_op | source)
XLA Modules:
  0.0 2087.1 jit_solution(15367808874646614422)
XLA Ops:
  14.3 44.8 %all-gather.10.cloned.1.call-done = bf16[512,3072]{0,1:T(8,128)(2,1)} async-done(((bf16[512,192]{0,1:T(8,128)(2,1)}), bf16[512,3072]{0,1:T(8,128)(2,1)}) %all-gather.10.cloned.1.call-update) | async-done | bytes 3145744 | tf_op jit(solution)/shard_map/all_gather | solution.py:110
  59.2 38.9 %all-gather.14.cloned.1.call-done = bf16[512,1024]{0,1:T(8,128)(2,1)} async-done(((bf16[512,64]{0,1:T(8,128)(2,1)}), bf16[512,1024]{0,1:T(8,128)(2,1)}) %all-gather.14.cloned.1.call-update) | async-done | bytes 1048592 | tf_op jit(solution)/shard_map/all_gather | solution.py:111
  98.1 54.9 %all-gather.18.cloned.1.call-done = bf16[512,4608]{0,1:T(8,128)(2,1)} async-done(((bf16[512,288]{0,1:T(8,128)(2,1)}), bf16[512,4608]{0,1:T(8,128)(2,1)}) %all-gather.18.cloned.1.call-update) | async-done | bytes 4718608 | tf_op jit(solution)/shard_map/all_gather | solution.py:112
  153.1 54.3 %all-gather.24.cloned.1.call-done = bf16[2304,1024]{0,1:T(8,128)(2,1)} async-done(((bf16[2304,64]{0,1:T(8,128)(2,1)}), bf16[2304,1024]{0,1:T(8,128)(2,1)}) %all-gather.24.cloned.1.call-update) | async-done | bytes 4718608 | tf_op jit(solution)/shard_map/all_gather | solution.py:114
  207.5 54.3 %all-gather.22.cloned.1.call-done = bf16[512,4608]{0,1:T(8,128)(2,1)} async-done(((bf16[512,288]{0,1:T(8,128)(2,1)}), bf16[512,4608]{0,1:T(8,128)(2,1)}) %all-gather.22.cloned.1.call-update) | async-done | bytes 4718608 | tf_op jit(solution)/shard_map/all_gather | solution.py:113
  263.4 183.1 %all_gather.33 = bf16[2,1024]{1,0:T(2,128)(2,1)S(1)} all-gather(bf16[2,512]{1,0:T(2,128)(2,1)S(1)} %convert_element_type.67), channel_id=1, replica_groups=mesh['dp'=16,'shard'=2] {'shard'}, dimensions={1}, use_global_device_ids=true | all-gather | bytes 6144 | tf_op jit(solution)/shard_map/all_gather | solution.py:126
  460.7 12.5 fusion.2
  473.2 101.2 %all-gather.20.cloned.1.call-done = bf16[1024,4608]{0,1:T(8,128)(2,1)} async-done(((bf16[512,4608]{0,1:T(8,128)(2,1)}), bf16[1024,4608]{0,1:T(8,128)(2,1)}) %all-gather.20.cloned.1.call-update) | async-done | bytes 9437200 | tf_op jit(solution)/shard_map/all_gather | solution.py:122
  574.4 8.3 fusion.53
  582.7 111.2 %all-gather.26.cloned.1.call-done = bf16[4608,1024]{0,1:T(8,128)(2,1)} async-done(((bf16[2304,1024]{0,1:T(8,128)(2,1)}), bf16[4608,1024]{0,1:T(8,128)(2,1)}) %all-gather.26.cloned.1.call-update) | async-done | bytes 9437200 | tf_op jit(solution)/shard_map/all_gather | solution.py:124
  694.0 6.6 fusion.54
  700.6 9.2 multiply_convert_fusion
  711.5 6.1 multiply_reduce_fusion
  725.9 6.4 fusion.28
  733.6 8.0 fusion.57
  741.7 8.2 fusion.56
  751.2 7.9 fusion.58
  764.9 10.9 reduce-scatter.24.cloned.1.call-done
  778.8 143.9 %reduce-scatter.22.cloned.1.call-done = f32[512,3072]{1,0:T(8,128)} async-done(((f32[1024,3072]{1,0:T(8,128)}), f32[512,3072]{1,0:T(8,128)}) %reduce-scatter.22.cloned.1.call-update) | async-done | bytes 6291472 | tf_op jit(solution)/shard_map/reduce_scatter | solution.py:69
  922.7 6.5 copy.153
  929.3 207.3 %reduce-scatter.28.cloned.1.call-done = f32[512,4608]{1,0:T(8,128)} async-done(((f32[1024,4608]{1,0:T(8,128)}), f32[512,4608]{1,0:T(8,128)}) %reduce-scatter.28.cloned.1.call-update) | async-done | bytes 9437200 | tf_op jit(solution)/shard_map/reduce_scatter | solution.py:69
  1136.6 9.6 copy.159
  1146.3 204.4 %reduce-scatter.26.cloned.1.call-done = f32[512,4608]{1,0:T(8,128)} async-done(((f32[1024,4608]{1,0:T(8,128)}), f32[512,4608]{1,0:T(8,128)}) %reduce-scatter.26.cloned.1.call-update) | async-done | bytes 9437200 | tf_op jit(solution)/shard_map/reduce_scatter | solution.py:69
  1350.7 9.6 copy.157
  1360.4 204.2 %reduce-scatter.30.cloned.1.call-done = f32[2304,1024]{1,0:T(8,128)} async-done(((f32[4608,1024]{1,0:T(8,128)}), f32[2304,1024]{1,0:T(8,128)}) %reduce-scatter.30.cloned.1.call-update) | async-done | bytes 9437200 | tf_op jit(solution)/shard_map/reduce_scatter | solution.py:69
  1564.7 9.6 copy.161
  1576.4 7.6 fusion.4
  1584.0 61.4 %psum.7 = f32[5,512]{1,0:T(8,128)S(1)} all-reduce(f32[5,512]{1,0:T(8,128)} %reduce-scatter.32.cloned.1.call-done), channel_id=1, replica_groups=mesh['dp'=16,'shard'=2] {'dp'}, use_global_device_ids=true, to_apply=%region_20.21 | all-reduce | flops 2560 | bytes 20480 | tf_op jit(solution)/shard_map/psum | solution.py:183
  1648.5 83.3 %reduce-scatter.34.cloned.1.call-done = f32[192,512]{1,0:T(8,128)} async-done(((f32[3072,512]{1,0:T(8,128)}), f32[192,512]{1,0:T(8,128)}) %reduce-scatter.34.cloned.1.call-update) | async-done | bytes 393232
  1734.3 112.5 %reduce-scatter.40.cloned.1.call-done = f32[288,512]{1,0:T(8,128)} async-done(((f32[4608,512]{1,0:T(8,128)}), f32[288,512]{1,0:T(8,128)}) %reduce-scatter.40.cloned.1.call-update) | async-done | bytes 589840
  1849.5 112.8 %reduce-scatter.38.cloned.1.call-done = f32[288,512]{1,0:T(8,128)} async-done(((f32[4608,512]{1,0:T(8,128)}), f32[288,512]{1,0:T(8,128)}) %reduce-scatter.38.cloned.1.call-update) | async-done | bytes 589840
  1965.1 112.6 %reduce-scatter.42.cloned.1.call-done = f32[64,2304]{1,0:T(8,128)} async-done(((f32[1024,2304]{1,0:T(8,128)}), f32[64,2304]{1,0:T(8,128)}) %reduce-scatter.42.cloned.1.call-update) | async-done | bytes 589840
  (196 shorter events, 59.9 us)
Async XLA Ops:
  7.2 51.9 %all-gather.10.cloned.1.call-start = ((), (), s32[]{:S(2)}) async-start(), calls=%async_computation.11 | async-start | bytes 3342336 | tf_op jit(solution)/shard_map/all_gather | solution.py:110
  9.1 89.0 %all-gather.14.cloned.1.call-start = ((), (), s32[]{:S(2)}) async-start(), calls=%async_computation.13 | async-start | bytes 1114112 | tf_op jit(solution)/shard_map/all_gather | solution.py:111
  10.7 142.4 %all-gather.18.cloned.1.call-start = ((), (), s32[]{:S(2)}) async-start(), calls=%async_computation.15 | async-start | bytes 5013504 | tf_op jit(solution)/shard_map/all_gather | solution.py:112
  12.6 194.9 %all-gather.24.cloned.1.call-start = ((), (), s32[]{:S(2)}) async-start(), calls=%async_computation.18 | async-start | bytes 5013504 | tf_op jit(solution)/shard_map/all_gather | solution.py:114
  13.4 248.4 %all-gather.22.cloned.1.call-start = ((), (), s32[]{:S(2)}) async-start(), calls=%async_computation.17 | async-start | bytes 5013504 | tf_op jit(solution)/shard_map/all_gather | solution.py:113
  14.3 437.2 %all-gather.12.cloned.1.call-start = ((), (), s32[]{:S(2)}) async-start(), calls=%async_computation.12 | async-start | bytes 9437184 | tf_op jit(solution)/shard_map/all_gather | solution.py:120
  59.1 398.5 %all-gather.16.cloned.1.call-start = ((), (), s32[]{:S(2)}) async-start(), calls=%async_computation.14 | async-start | bytes 3145728 | tf_op jit(solution)/shard_map/all_gather | solution.py:121
  98.1 476.3 %all-gather.20.cloned.1.call-start = ((), (), s32[]{:S(2)}) async-start(), calls=%async_computation.16 | async-start | bytes 14155776 | tf_op jit(solution)/shard_map/all_gather | solution.py:122
  153.1 540.9 %all-gather.26.cloned.1.call-start = ((), (), s32[]{:S(2)}) async-start(), calls=%async_computation.19 | async-start | bytes 14155776 | tf_op jit(solution)/shard_map/all_gather | solution.py:124
  207.5 243.8 %copy-start.4 = (bf16[128,1024]{1,0:T(8,128)(2,1)S(1)}, bf16[128,1024]{1,0:T(8,128)(2,1)}, u32[]{:S(2)}) copy-start(bf16[128,1024]{1,0:T(8,128)(2,1)} %param.23) | copy-start | bytes 786436
  207.5 568.3 %reduce-scatter.24.cloned.1.call-start = ((), (), s32[]{:S(2)}) async-start(), calls=%async_computation.21 | async-start | bytes 6291456 | tf_op jit(solution)/shard_map/reduce_scatter | solution.py:69
  261.9 198.5 %collective-permute-start = (bf16[512,4608]{0,1:T(8,128)(2,1)}, bf16[512,4608]{0,1:T(8,128)(2,1)}, u32[]{:S(2)}, u32[]{:S(2)}) collective-permute-start(bf16[512,4608]{0,1:T(8,128)(2,1)} %all-gather.22.cloned.1.call-done), channel_id=1, source_target_pairs={{0,1},{1,0},{2,3},{3,2},{4,5},{5,4},{6,7},{7,6},{8,9},{9,8},{10,11... | collective-permute-start | bytes 14155784 | tf_op jit(solution)/shard_map/ppermute | solution.py:24
  460.4 114.1 %copy-start.7 = (bf16[128,1024]{1,0:T(8,128)(2,1)}, bf16[128,1024]{1,0:T(8,128)(2,1)S(1)}, u32[]{:S(2)}) copy-start(bf16[128,1024]{1,0:T(8,128)(2,1)S(1)} %multiply_convert_fusion.6) | copy-start | bytes 786436
  473.2 220.7 %copy-start.10 = (bf16[128,1024]{1,0:T(8,128)(2,1)S(1)}, bf16[128,1024]{1,0:T(8,128)(2,1)}, u32[]{:S(2)}) copy-start(bf16[128,1024]{1,0:T(8,128)(2,1)} %param.24) | copy-start | bytes 786436
  721.3 201.4 %reduce-scatter.22.cloned.1.call-start = ((), (), s32[]{:S(2)}) async-start(), calls=%async_computation.20 | async-start | bytes 18874368 | tf_op jit(solution)/shard_map/reduce_scatter | solution.py:69
  732.4 404.3 %reduce-scatter.28.cloned.1.call-start = ((), (), s32[]{:S(2)}) async-start(), calls=%async_computation.23 | async-start | bytes 28311552 | tf_op jit(solution)/shard_map/reduce_scatter | solution.py:69
  741.7 609.1 %reduce-scatter.26.cloned.1.call-start = ((), (), s32[]{:S(2)}) async-start(), calls=%async_computation.22 | async-start | bytes 28311552 | tf_op jit(solution)/shard_map/reduce_scatter | solution.py:69
  749.9 814.8 %reduce-scatter.30.cloned.1.call-start = ((), (), s32[]{:S(2)}) async-start(), calls=%async_computation.24 | async-start | bytes 28311552 | tf_op jit(solution)/shard_map/reduce_scatter | solution.py:69
  759.2 824.8 %reduce-scatter.32.cloned.1.call-start = ((), (), s32[]{:S(2)}) async-start(), calls=%async_computation.25 | async-start | bytes 49152 | tf_op jit(solution)/shard_map/reduce_scatter | solution.py:182
  764.9 881.9 %reduce-scatter.36.cloned.1.call-start = ((), (), s32[]{:S(2)}) async-start(), calls=%async_computation.27 | async-start | bytes 2228224
  778.7 953.1 %reduce-scatter.34.cloned.1.call-start = ((), (), s32[]{:S(2)}) async-start(), calls=%async_computation.26 | async-start | bytes 6684672
  929.3 917.5 %reduce-scatter.40.cloned.1.call-start = ((), (), s32[]{:S(2)}) async-start(), calls=%async_computation.29 | async-start | bytes 10027008
  1146.3 816.1 %reduce-scatter.38.cloned.1.call-start = ((), (), s32[]{:S(2)}) async-start(), calls=%async_computation.28 | async-start | bytes 10027008
  1360.4 717.4 %reduce-scatter.42.cloned.1.call-start = ((), (), s32[]{:S(2)}) async-start(), calls=%async_computation.30 | async-start | bytes 10027008
  1576.4 155.4 %copy-start.21 = (f32[512,192]{0,1:T(8,128)S(1)}, f32[512,192]{0,1:T(8,128)}, u32[]{:S(2)}) copy-start(f32[512,192]{0,1:T(8,128)} %param.25) | copy-start | bytes 1179652
  1584.0 262.7 %copy-start.14 = (f32[512,288]{0,1:T(8,128)S(1)}, f32[512,288]{0,1:T(8,128)}, u32[]{:S(2)}) copy-start(f32[512,288]{0,1:T(8,128)} %param.28) | copy-start | bytes 1769476
  1584.0 262.7 %copy-start.28 = (f32[512,288]{0,1:T(8,128)S(1)}, f32[512,288]{0,1:T(8,128)}, u32[]{:S(2)}) copy-start(f32[512,288]{0,1:T(8,128)} %param.35) | copy-start | bytes 1769476
  1734.3 228.1 %copy-start.15 = (f32[512,288]{0,1:T(8,128)S(1)}, f32[512,288]{0,1:T(8,128)}, u32[]{:S(2)}) copy-start(f32[512,288]{0,1:T(8,128)} %param.27) | copy-start | bytes 1769476
  1734.3 228.1 %copy-start.29 = (f32[512,288]{0,1:T(8,128)S(1)}, f32[512,288]{0,1:T(8,128)}, u32[]{:S(2)}) copy-start(f32[512,288]{0,1:T(8,128)} %param.34) | copy-start | bytes 1769476
  1849.5 228.2 %copy-start.17 = (f32[2304,64]{0,1:T(8,128)S(1)}, f32[2304,64]{0,1:T(8,128)}, u32[]{:S(2)}) copy-start(f32[2304,64]{0,1:T(8,128)} %param.29) | copy-start | bytes 1769476
  1849.5 228.2 %copy-start.30 = (f32[2304,64]{0,1:T(8,128)S(1)}, f32[2304,64]{0,1:T(8,128)}, u32[]{:S(2)}) copy-start(f32[2304,64]{0,1:T(8,128)} %param.36) | copy-start | bytes 1769476
  1849.5 228.2 %copy-start.31 = (f32[2304,64]{0,1:T(8,128)S(1)}, f32[2304,64]{0,1:T(8,128)}, u32[]{:S(2)}) copy-start(f32[2304,64]{0,1:T(8,128)} %param.43) | copy-start | bytes 1769476
  (45 other events, 802.9 us)
Sparse Core Ops, SparseCore 0:
  10.9 48.1 all-gather.9
  61.8 36.1 all-gather.13
  100.9 52.0 all-gather.17
  155.8 51.6 all-gather.23
  210.2 51.6 all-gather.21
  263.3 146.3 all-gather.11
  411.2 45.0 all-gather.15
  457.9 116.5 all-gather.19
  576.0 117.9 all-gather.25
  721.4 54.3 reduce-scatter.23
  778.1 144.5 reduce-scatter.21
  924.9 211.7 reduce-scatter.27
  1138.9 211.7 reduce-scatter.25
  1352.9 211.7 reduce-scatter.29
  1567.3 9.9 reduce-scatter.31
  1581.5 61.8 reduce-scatter.35
  1647.8 84.0 reduce-scatter.33
  1736.4 110.3 reduce-scatter.39
  1851.4 110.8 reduce-scatter.37
  1966.9 110.8 reduce-scatter.41
